TPU v7x, 32 devices: a whole 2x2x4 slice. The times are simulated.
32 devices in a mesh: grp: 2 (over core), mr: 8 (over z, y), mc: 2 (over x).
Axes of the slice: x: 2, y: 2, z: 4, core: 2. Of those that a mesh axis runs over, the one named last changes fastest.
Arguments:
- queries: bfloat16 [384, 8192], P(('grp', 'mr'), 'mc'), may hold values from -6 to 6
- new_keys: bfloat16 [384, 1024], P(('grp', 'mr'), 'mc'), may hold values from -6 to 6
- new_values: bfloat16 [384, 1024], P(('grp', 'mr'), 'mc'), may hold values from -6 to 6
- key_cache: bfloat16 [384, 512, 1024], P(('grp', 'mr'), None, 'mc'), may hold values from -6 to 6
- value_cache: bfloat16 [384, 512, 1024], P(('grp', 'mr'), None, 'mc'), may hold values from -6 to 6
- context_len: int32 [384], P(('grp', 'mr')), may hold values from 2 to 512, as said below
- cache_slot: int32 [384], P(('grp', 'mr')), may hold values from 0 to 383, as said below
- residual_in: bfloat16 [384, 8192], P(('grp', 'mr'), 'mc'), may hold values from -31 to 31
- out_weight: bfloat16 [8192, 8192], P(('grp', 'mr'), 'mc'), may hold values from -0.25 to 0.25
- gate_weight: bfloat16 [8192, 28672], P('mc', ('grp', 'mr')), may hold values from -0.0625 to 0.0625
- up_weight: bfloat16 [8192, 28672], P('mc', ('grp', 'mr')), may hold values from -0.0625 to 0.0625
Outputs:
- residual_out: bfloat16 [384, 8192], P(('grp', 'mr'), 'mc')
- activation: bfloat16 [384, 28672], P('mc', ('grp', 'mr'))
Inputs may be any that keep to these rules, and one draw needn't show every extreme that they name: Row r's history fills positions 0 to context_len[r] - 1 of its cache row; some row has 512. `cache_slot`: within each aligned block of 24 rows the values are a permutation of that block's own row indices.
All inputs are finite; a program needn't handle non-finite values.
Results may differ from a plain program's by a relative error of at most 0.006.
Values may be sent and summed in bfloat16 or wider, within the bound.
A program may use at most 128 MiB of HBM per device.

v0:
```python
import jax
import jax.numpy as jnp
from jax import lax
from jax.sharding import PartitionSpec as P

D = 8192
HD = 128
norm_epsilon = 1e-05
masked_score = -1e30


def attend_rows(queries, new_keys, new_values, key_rows, value_rows, context_len):
    row_denominator_sum = queries.shape[0]
    context = key_rows.shape[1]
    kv_heads = key_rows.shape[2] // HD
    groups = queries.shape[1] // key_rows.shape[2]
    attention_logit_scale = HD ** (-0.5)
    query_grouped_four = queries.reshape(row_denominator_sum, kv_heads, groups, HD)
    key_four = key_rows.reshape(row_denominator_sum, context, kv_heads, HD)
    value_four = value_rows.reshape(row_denominator_sum, context, kv_heads, HD)
    current_key = new_keys.reshape(row_denominator_sum, kv_heads, HD)
    own_value = new_values.reshape(row_denominator_sum, kv_heads, HD).astype(jnp.float32)
    scores = (
        jnp.einsum(
            "bkgd,bckd->bkgc", query_grouped_four, key_four, preferred_element_type=jnp.float32
        )
        * attention_logit_scale
    )
    positions = jnp.arange(context, dtype=jnp.int32)
    valid_mask = positions[None, :] < context_len[:, None]
    scores = jnp.where(valid_mask[:, None, None, :], scores, masked_score)
    current_score = (
        jnp.einsum(
            "cnhz,cnz->cnh", query_grouped_four, current_key, preferred_element_type=jnp.float32
        )
        * attention_logit_scale
    )
    row_max = jnp.maximum(jnp.max(scores, axis=3), current_score)
    exponent = jnp.exp(scores - row_max[..., None])
    own_exponent = jnp.exp(current_score - row_max)
    denominator = jnp.sum(exponent, axis=3) + own_exponent
    weights = (exponent / denominator[..., None]).astype(jnp.bfloat16)
    own_weight = (own_exponent / denominator).astype(jnp.bfloat16).astype(jnp.float32)
    combined = jnp.einsum(
        "bkgc,bckd->bkgd", weights, value_four, preferred_element_type=jnp.float32
    )
    combined = combined + own_weight[..., None] * own_value[:, :, None, :]
    return combined.reshape(row_denominator_sum, -1).astype(jnp.bfloat16)


def body(
    queries,
    new_keys,
    new_values,
    key_cache,
    value_cache,
    context_len,
    cache_slot,
    residual_in,
    out_weight,
    gate_weight,
    up_weight,
):
    local_rows = queries.shape[0]
    row_base = lax.axis_index(("grp", "mr")) * local_rows
    device_slot_index = cache_slot - row_base
    positions = jnp.arange(local_rows, dtype=jnp.int32)
    matches = device_slot_index[:, None] == positions[None, :]
    inverse = jnp.sum(jnp.where(matches, positions[:, None], 0), axis=0)
    by_cache = attend_rows(
        jnp.take(queries, inverse, axis=0),
        jnp.take(new_keys, inverse, axis=0),
        jnp.take(new_values, inverse, axis=0),
        key_cache,
        value_cache,
        jnp.take(context_len, inverse, axis=0),
    )
    attended = jnp.take(by_cache, device_slot_index, axis=0)
    gathered = lax.all_gather(attended, "mc", axis=1, tiled=True)
    features = lax.all_to_all(gathered, ("grp", "mr"), split_axis=1, concat_axis=0, tiled=True)
    groups = lax.axis_size("grp")
    rows = features.shape[0]
    group_rows = rows // groups
    group = lax.axis_index("grp")
    own_share = None
    for shift in range(groups - 1, -1, -1):
        target = lax.rem(group + shift, groups)
        block = lax.dynamic_slice_in_dim(features, target * group_rows, group_rows, axis=0)
        term = jnp.dot(block, out_weight, preferred_element_type=jnp.float32)
        if shift > 0:
            pairs = [(i, (i + shift) % groups) for i in range(groups)]
            term = lax.ppermute(term.astype(jnp.bfloat16), "grp", pairs).astype(jnp.float32)
        own_share = term if own_share is None else own_share + term
    shares = lax.psum_scatter(
        own_share.astype(jnp.bfloat16), "mr", scatter_dimension=0, tiled=True
    ).astype(jnp.float32)
    residual_out = (residual_in.astype(jnp.float32) + shares).astype(jnp.bfloat16)
    group_part = lax.all_gather(residual_out, "mr", axis=0, tiled=True)
    everyone = lax.all_gather(group_part, "grp", axis=0, tiled=True) if groups != 2 else None
    if groups == 2:
        other_part = lax.ppermute(group_part, "grp", [(0, 1), (1, 0)])
        first = jnp.where(group == 0, group_part, other_part)
        second = jnp.where(group == 0, other_part, group_part)
        everyone = jnp.concatenate([first, second], axis=0)
    widened = lax.optimization_barrier(everyone).astype(jnp.float32)
    squares = jnp.sum(widened * widened, axis=1)
    square_sum = scatter_sum(squares, jnp.float32)
    gate_term = jnp.dot(everyone, gate_weight, preferred_element_type=jnp.float32)
    gate_sum = scatter_sum(gate_term, jnp.bfloat16)
    up_term = jnp.dot(everyone, up_weight, preferred_element_type=jnp.float32)
    up_sum = scatter_sum(up_term, jnp.bfloat16)
    inverse_rms = lax.rsqrt(square_sum / D + norm_epsilon)
    gate_value = gate_sum * inverse_rms[:, None]
    upward = up_sum * inverse_rms[:, None]
    activation = (jax.nn.silu(gate_value) * upward).astype(jnp.bfloat16)
    return (residual_out, activation)


def scatter_sum(term, kind):
    count = lax.axis_size("mc")
    me = lax.axis_index("mc")
    kept = term.shape[0] // count
    total = lax.dynamic_slice_in_dim(term, me * kept, kept, axis=0)
    for shift in range(1, count):
        target = lax.rem(me + shift, count)
        sent = lax.dynamic_slice_in_dim(term, target * kept, kept, axis=0).astype(kind)
        pairs = [(i, (i + shift) % count) for i in range(count)]
        total = total + lax.ppermute(sent, "mc", pairs).astype(jnp.float32)
    return total


def solution(mesh):
    in_specs = (
        P(("grp", "mr"), "mc"),
        P(("grp", "mr"), "mc"),
        P(("grp", "mr"), "mc"),
        P(("grp", "mr"), None, "mc"),
        P(("grp", "mr"), None, "mc"),
        P(("grp", "mr")),
        P(("grp", "mr")),
        P(("grp", "mr"), "mc"),
        P(("grp", "mr"), "mc"),
        P("mc", ("grp", "mr")),
        P("mc", ("grp", "mr")),
    )
    out_specs = (P(("grp", "mr"), "mc"), P("mc", ("grp", "mr")))
    return jax.shard_map(body, mesh=mesh, in_specs=in_specs, out_specs=out_specs, check_vma=False)
```

profile of v0, /device:TPU:0, one launch (start us, length us, event | category | flops | bytes accessed | tf_op | source)
XLA Modules:
  0.0 235.8 jit_solution(16639397591601032340)
XLA Ops:
  7.2 0.7 compare_and_fusion
  8.0 1.4 gather_fusion
  9.4 1.4 gather_fusion.2
  10.7 1.4 gather_fusion.3
  12.2 0.7 gather_fusion.1
  13.1 0.2 fusion.30
  13.3 6.5 %fusion.29 = (f32[24,4,8]{2,1,0:T(4,128)S(1)}, f32[24,4,8,512]{3,2,1,0:T(8,128)S(1)}) fusion(bf16[24,4,8,128]{3,2,1,0:T(8,128)(2,1)S(1)} %bitcast.56, pred[24,512]{1,0:T(8,128)(4,1)S(1)} %iota_compare_fusion, bf16[24,512,512]{2,1,0:T(8,128)(2,1)} %param.18), kind=kOutput, calls=%fused_computation.62 | convolution fusion | flops 101842176 | bytes 14367744 | tf_op jit(solution)/shard_map/bkgd,bckd->bkgc/dot_general | solution.py:24
  19.8 0.5 fusion.8
  20.4 5.8 %fusion.12 = bf16[24,4,8,128]{3,2,1,0:T(8,128)(2,1)S(1)} fusion(f32[24,4,8,512]{3,2,1,0:T(8,128)S(1)} %get-tuple-element.16, f32[24,4,8]{2,1,0:T(4,128)S(1)} %get-tuple-element.11, f32[24,4,8]{2,1,0:T(4,128)S(1)} %multiply_maximum_fusion, f32[24,4,128]{2,1,0:T(4,128)S(1)} %reshape.91, f32[24,4,8]{2,1,0:T(4,128)S(1)} %get-tuple-element.10, ...), kind=kOutput, calls=%fused_computation.25 | convolution fusion | flops 102137856 | bytes 14410752 | tf_op jit(solution)/shard_map/bkgc,bckd->bkgd/dot_general | solution.py:44
  26.3 0.7 gather_fusion.4
  27.1 8.5 %all_gather.6 = bf16[24,8192]{1,0:T(8,128)(2,1)S(1)} all-gather(bf16[24,4096]{1,0:T(8,128)(2,1)S(1)} %broadcast_select_fusion.2), channel_id=1, replica_groups=mesh['grp'=2,'mr'=8,'mc'=2] {'mc'}, dimensions={1}, use_global_device_ids=true | all-gather | bytes 589824 | tf_op jit(solution)/shard_map/all_gather | solution.py:79
  35.6 0.8 copy.46
  36.4 6.2 %all-to-all-start = ((bf16[24,16,512]{2,0,1:T(8,128)(2,1)}), bf16[24,16,512]{2,0,1:T(8,128)(2,1)S(1)}, u32[]{:S(2)}, u32[]{:S(2)}) async-start(bf16[24,16,512]{2,0,1:T(8,128)(2,1)} %bitcast.49), calls=%async_computation | async-start | bytes 786432 | tf_op jit(solution)/shard_map/all_to_all | solution.py:80
  42.6 13.0 %all-to-all-done = bf16[24,16,512]{2,0,1:T(8,128)(2,1)S(1)} async-done(((bf16[24,16,512]{2,0,1:T(8,128)(2,1)}), bf16[24,16,512]{2,0,1:T(8,128)(2,1)S(1)}, u32[]{:S(2)}, u32[]{:S(2)}) %all-to-all-start) | async-done | bytes 393248 | tf_op jit(solution)/shard_map/all_to_all | solution.py:80
  55.6 4.4 %convolution_convert_fusion = bf16[192,4096]{1,0:T(8,128)(2,1)} fusion(bf16[512,4096]{1,0:T(8,128)(2,1)} %param.23, bf16[384,512]{1,0:T(8,128)(2,1)S(1)} %bitcast.52, s32[]{:T(128)S(6)} %select_n.80), kind=kOutput, calls=%fused_computation.12 | convolution fusion | flops 806092800 | bytes 5963780 | tf_op jit(solution)/shard_map/dot_general | solution.py:89
  60.0 3.6 %collective-permute-done = bf16[192,4096]{1,0:T(8,128)(2,1)S(1)} collective-permute-done((bf16[192,4096]{1,0:T(8,128)(2,1)}, bf16[192,4096]{1,0:T(8,128)(2,1)S(1)}, u32[]{:S(2)}, u32[]{:S(2)}) %collective-permute-start) | collective-permute-done | bytes 1572896 | tf_op jit(solution)/shard_map/ppermute | solution.py:92
  63.6 4.4 %add_convert_fusion = bf16[192,4096]{1,0:T(8,128)(2,1)} fusion(bf16[192,4096]{1,0:T(8,128)(2,1)S(1)} %collective-permute-done, bf16[512,4096]{1,0:T(8,128)(2,1)} %param.23, bf16[384,512]{1,0:T(8,128)(2,1)S(1)} %bitcast.53, s32[]{:T(128)S(6)} %select_n.81), kind=kOutput, calls=%fused_computation.14 | convolution fusion | flops 807665664 | bytes 7536644 | tf_op jit(solution)/shard_map/dot_general | solution.py:89
  68.2 63.5 %reduce-scatter.2.cloned.1.call-done = bf16[24,4096]{1,0:T(8,128)(2,1)} async-done(((bf16[192,4096]{1,0:T(8,128)(2,1)}), bf16[24,4096]{1,0:T(8,128)(2,1)}) %reduce-scatter.2.cloned.1.call-update) | async-done | bytes 196624 | tf_op jit(solution)/shard_map/reduce_scatter | solution.py:94
  131.7 1.6 add_convert_fusion.1
  133.4 44.1 %all-gather.2.cloned.1.call-done = bf16[192,4096]{1,0:T(8,128)(2,1)} async-done(((bf16[24,4096]{1,0:T(8,128)(2,1)}), bf16[192,4096]{1,0:T(8,128)(2,1)}) %all-gather.2.cloned.1.call-update) | async-done | bytes 1572880 | tf_op jit(solution)/shard_map/all_gather | solution.py:98
  177.5 3.6 %collective-permute-done.1 = bf16[192,4096]{1,0:T(8,128)(2,1)S(1)} collective-permute-done((bf16[192,4096]{1,0:T(8,128)(2,1)}, bf16[192,4096]{1,0:T(8,128)(2,1)S(1)}, u32[]{:S(2)}, u32[]{:S(2)}) %collective-permute-start.1) | collective-permute-done | bytes 1572896 | tf_op jit(solution)/shard_map/ppermute | solution.py:101
  181.1 1.8 broadcast_select_fusion.1
  182.9 9.3 %fusion.28 = f32[384,1792]{1,0:T(8,128)S(1)} fusion(bf16[4096,1792]{1,0:T(8,128)(2,1)} %param.24, bf16[192,4096]{1,0:T(8,128)(2,1)S(1)} %get-tuple-element.9, bf16[192,4096]{1,0:T(8,128)(2,1)S(1)} %get-tuple-element.8), kind=kOutput, calls=%fused_computation.61 | convolution fusion | flops 5643436032 | bytes 20578304 | tf_op jit(solution)/shard_map/dot_general | solution.py:108
  192.2 0.9 dynamic-slice_convert_fusion.1
  193.2 1.5 collective-permute-start.2
  194.7 5.9 %fusion.27 = f32[384,1792]{1,0:T(8,128)S(1)} fusion(bf16[4096,1792]{1,0:T(8,128)(2,1)S(1)} %bitcast.61, bf16[192,4096]{1,0:T(8,128)(2,1)S(1)} %get-tuple-element.9, bf16[192,4096]{1,0:T(8,128)(2,1)S(1)} %get-tuple-element.8), kind=kOutput, calls=%fused_computation.60 | convolution fusion | flops 5643436032 | bytes 20578304 | tf_op jit(solution)/shard_map/dot_general | solution.py:110
  200.5 1.0 dynamic-slice_convert_fusion
  201.5 0.6 collective-permute-start.4
  202.3 0.7 multiply_reduce_fusion
  203.1 1.5 collective-permute-start.3
  204.6 21.1 %collective-permute-done.3 = f32[192]{0:T(256)S(1)} collective-permute-done((f32[192]{0:T(256)S(1)}, f32[192]{0:T(256)S(1)}, u32[]{:S(2)}, u32[]{:S(2)}) %collective-permute-start.3) | collective-permute-done | bytes 800 | tf_op jit(solution)/shard_map/ppermute | solution.py:128
  225.8 3.2 %multiply_convert_fusion = bf16[192,1792]{1,0:T(8,128)(2,1)} fusion(bf16[192,1792]{1,0:T(8,128)(2,1)} %collective-permute-done.4, f32[384,1792]{1,0:T(8,128)} %copy-done.2, s32[]{:T(128)S(6)} %select_n.85, bf16[192,1792]{1,0:T(8,128)(2,1)} %collective-permute-done.2, f32[384,1792]{1,0:T(8,128)S(1)} %fusion.28, f32[192]{0:T(256)S(1)} %add_rsqrt_fusion), kind=kLoop, calls=%fused_computation.21 | loop fusion | flops 4128768 | bytes 4817668 | tf_op jit(solution)/shard_map/convert_element_type | solution.py:115
  (44 shorter events, 1.4 us)
Async XLA Ops:
  7.2 5.0 %copy-start = (bf16[24,4096]{1,0:T(8,128)(2,1)S(1)}, bf16[24,4096]{1,0:T(8,128)(2,1)}, u32[]{:S(2)}) copy-start(bf16[24,4096]{1,0:T(8,128)(2,1)} %param.15) | copy-start | bytes 589828
  36.4 19.3 %all-to-all-start = ((bf16[24,16,512]{2,0,1:T(8,128)(2,1)}), bf16[24,16,512]{2,0,1:T(8,128)(2,1)S(1)}, u32[]{:S(2)}, u32[]{:S(2)}) async-start(bf16[24,16,512]{2,0,1:T(8,128)(2,1)} %bitcast.49), calls=%async_computation | async-start | bytes 786432 | tf_op jit(solution)/shard_map/all_to_all | solution.py:80
  42.5 89.1 %reduce-scatter.2.cloned.1.call-start = ((), (), s32[]{:S(2)}) async-start(), calls=%async_computation.2 | async-start | bytes 1769472 | tf_op jit(solution)/shard_map/reduce_scatter | solution.py:94
  60.0 3.6 %collective-permute-start = (bf16[192,4096]{1,0:T(8,128)(2,1)}, bf16[192,4096]{1,0:T(8,128)(2,1)S(1)}, u32[]{:S(2)}, u32[]{:S(2)}) collective-permute-start(bf16[192,4096]{1,0:T(8,128)(2,1)} %convolution_convert_fusion), channel_id=1, source_target_pairs={{0,16},{16,0},{1,17},{17,1},{2,18},{18,2},{3,19},{19,3},{4,20},{20... | collective-permute-start | bytes 4718600 | tf_op jit(solution)/shard_map/ppermute | solution.py:92
  60.0 71.7 %copy-start.3 = (bf16[24,4096]{1,0:T(8,128)(2,1)S(1)}, bf16[24,4096]{1,0:T(8,128)(2,1)}, u32[]{:S(2)}) copy-start(bf16[24,4096]{1,0:T(8,128)(2,1)} %param.22) | copy-start | bytes 589828
  68.0 109.5 %all-gather.2.cloned.1.call-start = ((), (), s32[]{:S(2)}) async-start(), calls=%async_computation.3 | async-start | bytes 1769472 | tf_op jit(solution)/shard_map/all_gather | solution.py:98
  177.5 3.6 %collective-permute-start.1 = (bf16[192,4096]{1,0:T(8,128)(2,1)}, bf16[192,4096]{1,0:T(8,128)(2,1)S(1)}, u32[]{:S(2)}, u32[]{:S(2)}) collective-permute-start(bf16[192,4096]{1,0:T(8,128)(2,1)} %all-gather.2.cloned.1.call-done), channel_id=1, source_target_pairs={{0,16},{16,0},{1,17},{17,1},{2,18},{18,2},{3,19},{19,3},{4,20},{20... | collective-permute-start | bytes 4718600 | tf_op jit(solution)/shard_map/ppermute | solution.py:101
  181.1 13.5 %slice-start = ((s8[14680064]{0:T(1024)(128)(4,1)}), s8[4194304]{0:T(1024)(128)(4,1)S(1)}, s32[]{:S(2)}) async-start(s8[14680064]{0:T(1024)(128)(4,1)} %bitcast.60), calls=%async_computation.4 | async-start | bytes 8388608
  182.9 11.7 %slice-start.1 = ((s8[14680064]{0:T(1024)(128)(4,1)}), s8[4194304]{0:T(1024)(128)(4,1)S(1)}, s32[]{:S(2)}) async-start(s8[14680064]{0:T(1024)(128)(4,1)} %bitcast.60), calls=%async_computation.5 | async-start | bytes 8388608
  182.9 11.7 %slice-start.2 = ((s8[14680064]{0:T(1024)(128)(4,1)}), s8[4194304]{0:T(1024)(128)(4,1)S(1)}, s32[]{:S(2)}) async-start(s8[14680064]{0:T(1024)(128)(4,1)} %bitcast.60), calls=%async_computation.6 | async-start | bytes 8388608
  182.9 11.7 %slice-start.3 = ((s8[14680064]{0:T(1024)(128)(4,1)}), s8[2097152]{0:T(1024)(128)(4,1)S(1)}, s32[]{:S(2)}) async-start(s8[14680064]{0:T(1024)(128)(4,1)} %bitcast.60), calls=%async_computation.7 | async-start | bytes 4194304
  193.2 32.6 %collective-permute-start.2 = (bf16[192,1792]{1,0:T(8,128)(2,1)}, bf16[192,1792]{1,0:T(8,128)(2,1)}, u32[]{:S(2)}, u32[]{:S(2)}) collective-permute-start(bf16[192,1792]{1,0:T(8,128)(2,1)} %dynamic-slice_convert_fusion.1), channel_id=1, source_target_pairs={{0,1},{1,0},{2,3},{3,2},{4,5},{5,4},{6,7},{7,6},{8,9},{9,8},{10,11... | collective-permute-start | bytes 2064392 | tf_op jit(solution)/shard_map/ppermute | solution.py:128
  200.5 1.8 copy-start.2
  201.5 24.3 %collective-permute-start.4 = (bf16[192,1792]{1,0:T(8,128)(2,1)}, bf16[192,1792]{1,0:T(8,128)(2,1)}, u32[]{:S(2)}, u32[]{:S(2)}) collective-permute-start(bf16[192,1792]{1,0:T(8,128)(2,1)} %dynamic-slice_convert_fusion), channel_id=1, source_target_pairs={{0,1},{1,0},{2,3},{3,2},{4,5},{5,4},{6,7},{7,6},{8,9},{9,8},{10,11... | collective-permute-start | bytes 2064392 | tf_op jit(solution)/shard_map/ppermute | solution.py:128
  202.3 26.7 %copy-start.1 = (bf16[24,4096]{1,0:T(8,128)(2,1)S(1)}, bf16[24,4096]{1,0:T(8,128)(2,1)}, u32[]{:S(2)}) copy-start(bf16[24,4096]{1,0:T(8,128)(2,1)} %param.15) | copy-start | bytes 589828
  203.1 22.6 %collective-permute-start.3 = (f32[192]{0:T(256)S(1)}, f32[192]{0:T(256)S(1)}, u32[]{:S(2)}, u32[]{:S(2)}) collective-permute-start(f32[192]{0:T(256)S(1)} %dynamic_slice.29), channel_id=1, source_target_pairs={{0,1},{1,0},{2,3},{3,2},{4,5},{5,4},{6,7},{7,6},{8,9},{9,8},{10,11... | collective-permute-start | bytes 2312 | tf_op jit(solution)/shard_map/ppermute | solution.py:128
Sparse Core Ops, SparseCore 0:
  68.1 63.5 reduce-scatter.1
  134.5 43.0 all-gather.1
where the time goes:
time: 236 us
  waiting for transfers between devices  149 us (63%)
  matrix products  36.3 us (15%)
  between operations  14.3 us (6%)
  starting transfers between devices  9.95 us (4%)
  other arithmetic  9.32 us (4%)
  blocking collectives  8.53 us (4%)
  local copies, waits for them, and re-layouts  8.38 us (4%)
    reduce_scatter x1, waiting for transfers between devices, body(): lax.psum_scatter(own_share.astype(jnp.bfloat16), 'mr', scatter_dimension=...  63.5 us
    all_gather x1, waiting for transfers between devices, body(): group_part = lax.all_gather(residual_out, 'mr', axis=0, tiled=True)  44.1 us
    ppermute x3, waiting for transfers between devices, scatter_sum(): total = total + lax.ppermute(sent, 'mc', pairs).astype(jnp.float32)  21.1 us
    all_to_all x1, waiting for transfers between devices, body(): lax.all_to_all(gathered, ('grp', 'mr'), split_axis=1, concat_axis=0, tile...  13 us
    dot_general x1, matrix products, body(): jnp.dot(everyone, gate_weight, preferred_element_type=jnp.float32)  9.31 us
    dot_general x2, matrix products, body(): term = jnp.dot(block, out_weight, preferred_element_type=jnp.float32)  8.72 us
    all_gather x1, blocking collectives, body(): gathered = lax.all_gather(attended, 'mc', axis=1, tiled=True)  8.53 us
    dot_general x1, matrix products, attend_rows(): jnp.einsum('bkgd,bckd->bkgc', query_grouped_four, key_four, preferred_ele...  6.45 us
  transfers between devices with their start and end apart: 8, of which 6 were waited for; matrix products, arithmetic and copies ran while one was open for 3% of the time, Pallas kernels for 0%

commit v1 on v0

--- a/solution.py
+++ b/solution.py
@@ -95,7 +95,9 @@
         own_share.astype(jnp.bfloat16), "mr", scatter_dimension=0, tiled=True
     ).astype(jnp.float32)
     residual_out = (residual_in.astype(jnp.float32) + shares).astype(jnp.bfloat16)
-    group_part = lax.all_gather(residual_out, "mr", axis=0, tiled=True)
+    group_part = jnp.concatenate(
+        lax.all_to_all(jnp.stack([residual_out] * lax.axis_size("mr")), "mr", 0, 0), axis=0
+    )
     everyone = lax.all_gather(group_part, "grp", axis=0, tiled=True) if groups != 2 else None
     if groups == 2:
         other_part = lax.ppermute(group_part, "grp", [(0, 1), (1, 0)])

time: 236 us -> 229 us (0.970)
  waiting for transfers between devices: 149 us -> 105 us
  blocking collectives: 8.53 us -> 47.4 us
    all_gather x1 -> x0, waiting for transfers between devices: 44.1 us -> none  [body(): group_part = lax.all_gather(residual_out, 'mr', axis=0, tiled=True)]
    all_to_all x0 -> x1, blocking collectives: none -> 38.9 us  [body(): lax.all_to_all(jnp.stack([residual_out] * lax.axis_size('mr')), 'mr', 0, 0)]
  transfers between devices with their start and end apart: 8 -> 7, of which waited for: 6 -> 5; matrix products, arithmetic and copies ran while one was open for 3% -> 3% of each run, Pallas kernels for 0% -> 0%
where the time goes in v1:
time: 229 us
  waiting for transfers between devices  105 us (46%)
  blocking collectives  47.4 us (21%)
  matrix products  36.3 us (16%)
  between operations  14.3 us (6%)
  starting transfers between devices  9.75 us (4%)
  local copies, waits for them, and re-layouts  8.53 us (4%)
  other arithmetic  7.18 us (3%)
    reduce_scatter x1, waiting for transfers between devices, body(): lax.psum_scatter(own_share.astype(jnp.bfloat16), 'mr', scatter_dimension=...  63.8 us
    all_to_all x1, blocking collectives, body(): lax.all_to_all(jnp.stack([residual_out] * lax.axis_size('mr')), 'mr', 0, 0)  38.9 us
    ppermute x3, waiting for transfers between devices, scatter_sum(): total = total + lax.ppermute(sent, 'mc', pairs).astype(jnp.float32)  21.1 us
    all_to_all x1, waiting for transfers between devices, body(): lax.all_to_all(gathered, ('grp', 'mr'), split_axis=1, concat_axis=0, tile...  13 us
    dot_general x1, matrix products, body(): jnp.dot(everyone, gate_weight, preferred_element_type=jnp.float32)  9.34 us
    dot_general x2, matrix products, body(): term = jnp.dot(block, out_weight, preferred_element_type=jnp.float32)  8.7 us
    all_gather x1, blocking collectives, body(): gathered = lax.all_gather(attended, 'mc', axis=1, tiled=True)  8.53 us
    dot_general x1, matrix products, attend_rows(): jnp.einsum('bkgd,bckd->bkgc', query_grouped_four, key_four, preferred_ele...  6.45 us
  transfers between devices with their start and end apart: 7, of which 5 were waited for; matrix products, arithmetic and copies ran while one was open for 3% of the time, Pallas kernels for 0%

profile of v1, /device:TPU:0, one launch (start us, length us, event | category | flops | bytes accessed | tf_op | source)
XLA Modules:
  0.0 228.5 jit_solution(16923854433786790951)
XLA Ops:
  7.2 0.7 compare_and_fusion
  8.0 1.4 gather_fusion
  9.4 1.4 gather_fusion.2
  10.7 1.4 gather_fusion.3
  12.2 0.7 gather_fusion.1
  13.1 0.2 fusion.30
  13.3 6.5 %fusion.29 = (f32[24,4,8]{2,1,0:T(4,128)S(1)}, f32[24,4,8,512]{3,2,1,0:T(8,128)S(1)}) fusion(bf16[24,4,8,128]{3,2,1,0:T(8,128)(2,1)S(1)} %bitcast.60, pred[24,512]{1,0:T(8,128)(4,1)S(1)} %iota_compare_fusion, bf16[24,512,512]{2,1,0:T(8,128)(2,1)} %param.18), kind=kOutput, calls=%fused_computation.62 | convolution fusion | flops 101842176 | bytes 14367744 | tf_op jit(solution)/shard_map/bkgd,bckd->bkgc/dot_general | solution.py:24
  19.8 0.5 fusion.8
  20.4 5.8 %fusion.12 = bf16[24,4,8,128]{3,2,1,0:T(8,128)(2,1)S(1)} fusion(f32[24,4,8,512]{3,2,1,0:T(8,128)S(1)} %get-tuple-element.16, f32[24,4,8]{2,1,0:T(4,128)S(1)} %get-tuple-element.11, f32[24,4,8]{2,1,0:T(4,128)S(1)} %multiply_maximum_fusion, f32[24,4,128]{2,1,0:T(4,128)S(1)} %reshape.97, f32[24,4,8]{2,1,0:T(4,128)S(1)} %get-tuple-element.10, ...), kind=kOutput, calls=%fused_computation.25 | convolution fusion | flops 102137856 | bytes 14410752 | tf_op jit(solution)/shard_map/bkgc,bckd->bkgd/dot_general | solution.py:44
  26.3 0.7 gather_fusion.4
  27.1 8.5 %all_gather.3 = bf16[24,8192]{1,0:T(8,128)(2,1)S(1)} all-gather(bf16[24,4096]{1,0:T(8,128)(2,1)S(1)} %broadcast_select_fusion.2), channel_id=1, replica_groups=mesh['grp'=2,'mr'=8,'mc'=2] {'mc'}, dimensions={1}, use_global_device_ids=true | all-gather | bytes 589824 | tf_op jit(solution)/shard_map/all_gather | solution.py:79
  35.6 0.8 copy.46
  36.4 6.2 %all-to-all-start = ((bf16[24,16,512]{2,0,1:T(8,128)(2,1)}), bf16[24,16,512]{2,0,1:T(8,128)(2,1)S(1)}, u32[]{:S(2)}, u32[]{:S(2)}) async-start(bf16[24,16,512]{2,0,1:T(8,128)(2,1)} %bitcast.52), calls=%async_computation | async-start | bytes 786432 | tf_op jit(solution)/shard_map/all_to_all | solution.py:80
  42.6 13.0 %all-to-all-done = bf16[24,16,512]{2,0,1:T(8,128)(2,1)S(1)} async-done(((bf16[24,16,512]{2,0,1:T(8,128)(2,1)}), bf16[24,16,512]{2,0,1:T(8,128)(2,1)S(1)}, u32[]{:S(2)}, u32[]{:S(2)}) %all-to-all-start) | async-done | bytes 393248 | tf_op jit(solution)/shard_map/all_to_all | solution.py:80
  55.6 4.3 %convolution_convert_fusion = bf16[192,4096]{1,0:T(8,128)(2,1)} fusion(bf16[512,4096]{1,0:T(8,128)(2,1)} %param.23, bf16[384,512]{1,0:T(8,128)(2,1)S(1)} %bitcast.56, s32[]{:T(128)S(6)} %select_n.80), kind=kOutput, calls=%fused_computation.12 | convolution fusion | flops 806092800 | bytes 5963780 | tf_op jit(solution)/shard_map/dot_general | solution.py:89
  60.0 3.6 %collective-permute-done = bf16[192,4096]{1,0:T(8,128)(2,1)S(1)} collective-permute-done((bf16[192,4096]{1,0:T(8,128)(2,1)}, bf16[192,4096]{1,0:T(8,128)(2,1)S(1)}, u32[]{:S(2)}, u32[]{:S(2)}) %collective-permute-start) | collective-permute-done | bytes 1572896 | tf_op jit(solution)/shard_map/ppermute | solution.py:92
  63.6 4.4 %add_convert_fusion = bf16[192,4096]{1,0:T(8,128)(2,1)} fusion(bf16[192,4096]{1,0:T(8,128)(2,1)S(1)} %collective-permute-done, bf16[512,4096]{1,0:T(8,128)(2,1)} %param.23, bf16[384,512]{1,0:T(8,128)(2,1)S(1)} %bitcast.57, s32[]{:T(128)S(6)} %select_n.81), kind=kOutput, calls=%fused_computation.14 | convolution fusion | flops 807665664 | bytes 7536644 | tf_op jit(solution)/shard_map/dot_general | solution.py:89
  68.0 63.8 %reduce-scatter.2.cloned.1.call-done = bf16[24,4096]{1,0:T(8,128)(2,1)} async-done(((bf16[192,4096]{1,0:T(8,128)(2,1)}), bf16[24,4096]{1,0:T(8,128)(2,1)}) %reduce-scatter.2.cloned.1.call-update) | async-done | bytes 196624 | tf_op jit(solution)/shard_map/reduce_scatter | solution.py:94
  131.7 1.0 add_convert_fusion.1
  132.9 38.9 %all_to_all.24 = bf16[8,24,4096]{2,1,0:T(8,128)(2,1)S(1)} all-to-all(bf16[8,24,4096]{2,1,0:T(8,128)(2,1)S(1)} %stack.2), channel_id=1, replica_groups=mesh['grp'=2,'mr'=8,'mc'=2] {'mr'}, dimensions={0} | all-to-all | bytes 3145728 | tf_op jit(solution)/shard_map/all_to_all | solution.py:99
  171.8 3.4 %collective-permute-done.1 = bf16[192,4096]{1,0:T(8,128)(2,1)S(1)} collective-permute-done((bf16[192,4096]{1,0:T(8,128)(2,1)S(1)}, bf16[192,4096]{1,0:T(8,128)(2,1)S(1)}, u32[]{:S(2)}, u32[]{:S(2)}) %collective-permute-start.1) | collective-permute-done | bytes 1572896 | tf_op jit(solution)/shard_map/ppermute | solution.py:103
  175.2 0.3 broadcast_select_fusion.1
  175.6 9.3 %fusion.28 = f32[384,1792]{1,0:T(8,128)S(1)} fusion(bf16[4096,1792]{1,0:T(8,128)(2,1)} %param.24, bf16[192,4096]{1,0:T(8,128)(2,1)S(1)} %get-tuple-element.9, bf16[192,4096]{1,0:T(8,128)(2,1)S(1)} %get-tuple-element.8), kind=kOutput, calls=%fused_computation.61 | convolution fusion | flops 5643436032 | bytes 20578304 | tf_op jit(solution)/shard_map/dot_general | solution.py:110
  184.9 0.9 dynamic-slice_convert_fusion.1
  185.9 1.5 collective-permute-start.2
  187.4 5.9 %fusion.27 = f32[384,1792]{1,0:T(8,128)S(1)} fusion(bf16[4096,1792]{1,0:T(8,128)(2,1)S(1)} %bitcast.65, bf16[192,4096]{1,0:T(8,128)(2,1)S(1)} %get-tuple-element.9, bf16[192,4096]{1,0:T(8,128)(2,1)S(1)} %get-tuple-element.8), kind=kOutput, calls=%fused_computation.60 | convolution fusion | flops 5643436032 | bytes 20578304 | tf_op jit(solution)/shard_map/dot_general | solution.py:112
  193.2 1.0 dynamic-slice_convert_fusion
  194.2 0.5 collective-permute-start.4
  195.0 0.7 multiply_reduce_fusion
  195.8 1.5 collective-permute-start.3
  197.3 21.1 %collective-permute-done.3 = f32[192]{0:T(256)S(1)} collective-permute-done((f32[192]{0:T(256)S(1)}, f32[192]{0:T(256)S(1)}, u32[]{:S(2)}, u32[]{:S(2)}) %collective-permute-start.3) | collective-permute-done | bytes 800 | tf_op jit(solution)/shard_map/ppermute | solution.py:130
  218.5 3.2 %multiply_convert_fusion = bf16[192,1792]{1,0:T(8,128)(2,1)} fusion(bf16[192,1792]{1,0:T(8,128)(2,1)} %collective-permute-done.4, f32[384,1792]{1,0:T(8,128)} %copy-done.2, s32[]{:T(128)S(6)} %select_n.85, bf16[192,1792]{1,0:T(8,128)(2,1)} %collective-permute-done.2, f32[384,1792]{1,0:T(8,128)S(1)} %fusion.28, f32[192]{0:T(256)S(1)} %add_rsqrt_fusion), kind=kLoop, calls=%fused_computation.21 | loop fusion | flops 4128768 | bytes 4817668 | tf_op jit(solution)/shard_map/convert_element_type | solution.py:117
  (45 shorter events, 1.3 us)
Async XLA Ops:
  7.2 5.0 %copy-start = (bf16[24,4096]{1,0:T(8,128)(2,1)S(1)}, bf16[24,4096]{1,0:T(8,128)(2,1)}, u32[]{:S(2)}) copy-start(bf16[24,4096]{1,0:T(8,128)(2,1)} %param.15) | copy-start | bytes 589828
  36.4 19.3 %all-to-all-start = ((bf16[24,16,512]{2,0,1:T(8,128)(2,1)}), bf16[24,16,512]{2,0,1:T(8,128)(2,1)S(1)}, u32[]{:S(2)}, u32[]{:S(2)}) async-start(bf16[24,16,512]{2,0,1:T(8,128)(2,1)} %bitcast.52), calls=%async_computation | async-start | bytes 786432 | tf_op jit(solution)/shard_map/all_to_all | solution.py:80
  42.6 89.2 %reduce-scatter.2.cloned.1.call-start = ((), (), s32[]{:S(2)}) async-start(), calls=%async_computation.3 | async-start | bytes 1769472 | tf_op jit(solution)/shard_map/reduce_scatter | solution.py:94
  60.0 3.6 %collective-permute-start = (bf16[192,4096]{1,0:T(8,128)(2,1)}, bf16[192,4096]{1,0:T(8,128)(2,1)S(1)}, u32[]{:S(2)}, u32[]{:S(2)}) collective-permute-start(bf16[192,4096]{1,0:T(8,128)(2,1)} %convolution_convert_fusion), channel_id=1, source_target_pairs={{0,16},{16,0},{1,17},{17,1},{2,18},{18,2},{3,19},{19,3},{4,20},{20... | collective-permute-start | bytes 4718600 | tf_op jit(solution)/shard_map/ppermute | solution.py:92
  60.0 71.8 %copy-start.4 = (bf16[24,4096]{1,0:T(8,128)(2,1)S(1)}, bf16[24,4096]{1,0:T(8,128)(2,1)}, u32[]{:S(2)}) copy-start(bf16[24,4096]{1,0:T(8,128)(2,1)} %param.22) | copy-start | bytes 589828
  132.7 42.8 %copy-start.3 = (bf16[24,4096]{1,0:T(8,128)(2,1)}, bf16[24,4096]{1,0:T(8,128)(2,1)S(1)}, u32[]{:S(2)}) copy-start(bf16[24,4096]{1,0:T(8,128)(2,1)S(1)} %add_convert_fusion.1) | copy-start | bytes 589828
  171.8 3.4 %collective-permute-start.1 = (bf16[192,4096]{1,0:T(8,128)(2,1)S(1)}, bf16[192,4096]{1,0:T(8,128)(2,1)S(1)}, u32[]{:S(2)}, u32[]{:S(2)}) collective-permute-start(bf16[192,4096]{1,0:T(8,128)(2,1)S(1)} %bitcast.55), channel_id=1, source_target_pairs={{0,16},{16,0},{1,17},{17,1},{2,18},{18,2},{3,19},{19,3},{4,20},{20... | collective-permute-start | bytes 4718600 | tf_op jit(solution)/shard_map/ppermute | solution.py:103
  175.2 12.1 %slice-start = ((s8[14680064]{0:T(1024)(128)(4,1)}), s8[4194304]{0:T(1024)(128)(4,1)S(1)}, s32[]{:S(2)}) async-start(s8[14680064]{0:T(1024)(128)(4,1)} %bitcast.64), calls=%async_computation.4 | async-start | bytes 8388608
  175.5 11.8 %slice-start.1 = ((s8[14680064]{0:T(1024)(128)(4,1)}), s8[4194304]{0:T(1024)(128)(4,1)S(1)}, s32[]{:S(2)}) async-start(s8[14680064]{0:T(1024)(128)(4,1)} %bitcast.64), calls=%async_computation.5 | async-start | bytes 8388608
  175.6 11.8 %slice-start.2 = ((s8[14680064]{0:T(1024)(128)(4,1)}), s8[4194304]{0:T(1024)(128)(4,1)S(1)}, s32[]{:S(2)}) async-start(s8[14680064]{0:T(1024)(128)(4,1)} %bitcast.64), calls=%async_computation.6 | async-start | bytes 8388608
  175.6 11.8 %slice-start.3 = ((s8[14680064]{0:T(1024)(128)(4,1)}), s8[2097152]{0:T(1024)(128)(4,1)S(1)}, s32[]{:S(2)}) async-start(s8[14680064]{0:T(1024)(128)(4,1)} %bitcast.64), calls=%async_computation.7 | async-start | bytes 4194304
  185.9 32.6 %collective-permute-start.2 = (bf16[192,1792]{1,0:T(8,128)(2,1)}, bf16[192,1792]{1,0:T(8,128)(2,1)}, u32[]{:S(2)}, u32[]{:S(2)}) collective-permute-start(bf16[192,1792]{1,0:T(8,128)(2,1)} %dynamic-slice_convert_fusion.1), channel_id=1, source_target_pairs={{0,1},{1,0},{2,3},{3,2},{4,5},{5,4},{6,7},{7,6},{8,9},{9,8},{10,11... | collective-permute-start | bytes 2064392 | tf_op jit(solution)/shard_map/ppermute | solution.py:130
  193.2 1.8 copy-start.2
  194.2 24.2 %collective-permute-start.4 = (bf16[192,1792]{1,0:T(8,128)(2,1)}, bf16[192,1792]{1,0:T(8,128)(2,1)}, u32[]{:S(2)}, u32[]{:S(2)}) collective-permute-start(bf16[192,1792]{1,0:T(8,128)(2,1)} %dynamic-slice_convert_fusion), channel_id=1, source_target_pairs={{0,1},{1,0},{2,3},{3,2},{4,5},{5,4},{6,7},{7,6},{8,9},{9,8},{10,11... | collective-permute-start | bytes 2064392 | tf_op jit(solution)/shard_map/ppermute | solution.py:130
  195.0 26.7 %copy-start.1 = (bf16[24,4096]{1,0:T(8,128)(2,1)S(1)}, bf16[24,4096]{1,0:T(8,128)(2,1)}, u32[]{:S(2)}) copy-start(bf16[24,4096]{1,0:T(8,128)(2,1)} %param.15) | copy-start | bytes 589828
  195.8 22.6 %collective-permute-start.3 = (f32[192]{0:T(256)S(1)}, f32[192]{0:T(256)S(1)}, u32[]{:S(2)}, u32[]{:S(2)}) collective-permute-start(f32[192]{0:T(256)S(1)} %dynamic_slice.29), channel_id=1, source_target_pairs={{0,1},{1,0},{2,3},{3,2},{4,5},{5,4},{6,7},{7,6},{8,9},{9,8},{10,11... | collective-permute-start | bytes 2312 | tf_op jit(solution)/shard_map/ppermute | solution.py:130
Sparse Core Ops, SparseCore 0:
  68.1 63.6 reduce-scatter.1
